TPU v7x, 128 devices: a whole 4x4x4 slice. The times are simulated.
128 devices in a mesh: ctx: 8 (over y, core), fsdp: 16 (over x, z).
Axes of the slice: x: 4, y: 4, z: 4, core: 2. Of those that a mesh axis runs over, the one named last changes fastest.
Arguments:
- hidden: bfloat16 [8, 16, 256, 2048], P('ctx', 'fsdp'), may hold values from -4.5 to 4.5
- norm_gain: float32 [2048], replicated, may hold values from 0.1 to 1.9
- w_query: bfloat16 [2048, 2048], P('fsdp', 'ctx'), may hold values from -1 to 1
- w_key: bfloat16 [2048, 1024], P('fsdp', 'ctx'), may hold values from -1 to 1
- w_value: bfloat16 [2048, 1024], P('fsdp', 'ctx'), may hold values from -0.125 to 0.125
- q_gain: float32 [128], replicated, may hold values from 0.5 to 5
- k_gain: float32 [128], replicated, may hold values from 0.5 to 5
- lengths: int32 [16, 4], replicated, may hold values from 1 to 1024, 2048 in all within a row
- piece_map: int32 [16, 8], replicated, may hold values from 0 to 7, each once within a row
- owner: int32 [8, 16, 256], P('ctx', 'fsdp'), may hold values from 0 to 127, as said below
- slot: int32 [8, 16, 256], P('ctx', 'fsdp'), may hold values from 0 to 511, as said below
Outputs:
- attended: bfloat16 [8, 16, 256, 2048], P('ctx', 'fsdp')
- cache: bfloat16 [65536, 2048], P(('ctx', 'fsdp'))
Inputs may be any that keep to these rules, and one draw needn't show every extreme that they name: `lengths`: each row sums to 2048; its largest entry is 1024. `piece_map`: each row holds every piece once. At most 4 tokens of one device go to one owner; in every draw one owner receives exactly 4 from every device. `slot`: tokens with the same owner have distinct slots.
All inputs are finite; a program needn't handle non-finite values.
Results may differ from a plain program's by a relative error of at most 0.0035.
The roundings to bfloat16 on the way count: a program that leaves them out, or rounds other values in their place, can miss the bound.
Values may be sent and summed in bfloat16 or wider, within the bound.
No kernel may reach another device: no remote copies, remote signals or barrier semaphores. Data moves between devices by JAX's collectives and lax.ppermute only.
A program may use at most 128 MiB of HBM per device.

v0:
```python
import math
import jax
import jax.numpy as jnp
from jax import lax
from jax.sharding import PartitionSpec as P

HEAD_WIDTH = 128
EPSILON = 1e-06
THETA = 1000000.0
NEG_BIG = -1e30


def norm_rope(projected, gain_vec, relative, head_size):
    row_count = projected.shape[0]
    head_count = projected.shape[1] // head_size
    shaped = projected.reshape(row_count, head_count, head_size)
    factor = lax.rsqrt(jnp.mean(shaped * shaped, axis=-1, keepdims=True) + EPSILON)
    normal = shaped * factor * gain_vec
    half_size = head_size // 2
    frequency = jnp.exp(
        jnp.arange(half_size, dtype=jnp.float32) * (-2.0 * math.log(THETA) / head_size)
    )
    angles = relative.astype(jnp.float32)[:, None] * frequency[None, :]
    cosine = jnp.cos(angles)[:, None, :]
    sine_part = jnp.sin(angles)[:, None, :]
    first_half = normal[..., :half_size]
    second = normal[..., half_size:]
    turned = jnp.concatenate(
        [first_half * cosine - second * sine_part, second * cosine + first_half * sine_part],
        axis=-1,
    )
    return turned.reshape(row_count, head_count * head_size).astype(jnp.bfloat16)


def attend_keys(
    state_tuple, heads_of_query, query_pos, query_seg, key_rows, value_rows, key_pos, key_seg
):
    row_max, row_sum, weighted = state_tuple
    heads_of_key = key_rows.reshape(key_rows.shape[0], -1, HEAD_WIDTH)
    heads_of_value = value_rows.reshape(value_rows.shape[0], -1, HEAD_WIDTH)
    scores = jnp.einsum(
        "tkgd,skd->tkgs", heads_of_query, heads_of_key, preferred_element_type=jnp.float32
    ) * (1.0 / math.sqrt(HEAD_WIDTH))
    visible = ((query_seg[:, None] == key_seg[None, :]) & (key_pos[None, :] <= query_pos[:, None]))[
        :, None, None, :
    ]
    masked = jnp.where(visible, scores, NEG_BIG)
    new_max = jnp.maximum(row_max, jnp.max(masked, axis=-1))
    weights = jnp.where(visible, jnp.exp(masked - new_max[..., None]), 0.0)
    shrink = jnp.exp(row_max - new_max)
    row_sum = row_sum * shrink + jnp.sum(weights, axis=-1)
    weighted = weighted * shrink[..., None] + jnp.einsum(
        "tkgs,skd->tkgd",
        weights.astype(jnp.bfloat16),
        heads_of_value,
        preferred_element_type=jnp.float32,
    )
    return (new_max, row_sum, weighted)


def sweep_keys(
    state_tuple, heads_of_query, query_pos, query_seg, key_rows, value_rows, key_pos, key_seg
):
    row_span = key_rows.shape[0]
    key_block = 512
    steps_count = row_span // key_block

    def step_keys(carried, key_items):
        return (
            attend_keys(
                carried,
                heads_of_query,
                query_pos,
                query_seg,
                key_items[0],
                key_items[1],
                key_items[2],
                key_items[3],
            ),
            None,
        )

    result_carry, unused = lax.scan(
        step_keys,
        state_tuple,
        (
            key_rows.reshape(steps_count, key_block, -1),
            value_rows.reshape(steps_count, key_block, -1),
            key_pos.reshape(steps_count, key_block),
            key_seg.reshape(steps_count, key_block),
        ),
    )
    return result_carry


def empty_state(row_count, kv_heads, group_width):
    return (
        jnp.full((row_count, kv_heads, group_width), NEG_BIG, jnp.float32),
        jnp.zeros((row_count, kv_heads, group_width), jnp.float32),
        jnp.zeros((row_count, kv_heads, group_width, HEAD_WIDTH), jnp.float32),
    )


def project_rows(source, pieces):
    return tuple(
        (jnp.dot(source, shard_rows, preferred_element_type=jnp.float32) for shard_rows in pieces)
    )


def shards(
    hidden, norm_gain, w_query, w_key, w_value, q_gain, k_gain, lengths, piece_map, owner, slot
):
    tok_rows = hidden.shape[2]
    ctx_count = lax.axis_size("ctx")
    fsdp_count = lax.axis_size("fsdp")
    owner_count = ctx_count * fsdp_count
    group_index = lax.axis_index("fsdp")
    ctx_index = lax.axis_index("ctx")
    inputs = hidden[0, 0].astype(jnp.float32)
    factor = lax.rsqrt(jnp.mean(inputs * inputs, axis=-1, keepdims=True) + EPSILON)
    normed = (inputs * factor * norm_gain).astype(jnp.bfloat16)
    my_lengths = lax.dynamic_index_in_dim(lengths, group_index, 0, keepdims=False)
    my_pieces = lax.dynamic_index_in_dim(piece_map, group_index, 0, keepdims=False)
    seg_ends = jnp.cumsum(my_lengths, dtype=jnp.int32)
    starts = seg_ends - my_lengths
    seg_count = lengths.shape[1]

    def stream_info(row_ids):
        holder = row_ids // tok_rows
        piece_ids = jnp.sum(
            jnp.where(
                holder[:, None] == jnp.arange(ctx_count, dtype=jnp.int32)[None, :],
                my_pieces[None, :],
                0,
            ),
            axis=1,
            dtype=jnp.int32,
        )
        positions = piece_ids * tok_rows + row_ids % tok_rows
        segment = jnp.sum(
            (positions[:, None] >= seg_ends[None, :]).astype(jnp.int32), axis=1, dtype=jnp.int32
        )
        relative = positions - jnp.sum(
            jnp.where(
                segment[:, None] == jnp.arange(seg_count, dtype=jnp.int32)[None, :],
                starts[None, :],
                0,
            ),
            axis=1,
            dtype=jnp.int32,
        )
        return (positions, segment, relative)

    query_cols, key_cols, value_cols = (
        lax.all_gather(w_query, "ctx", axis=1, tiled=True),
        lax.all_gather(w_key, "ctx", axis=1, tiled=True),
        lax.all_gather(w_value, "ctx", axis=1, tiled=True),
    )
    query_raw, key_raw, value_raw = project_rows(
        normed,
        (
            lax.all_gather(query_cols, "fsdp", axis=0, tiled=True),
            lax.all_gather(key_cols, "fsdp", axis=0, tiled=True),
            lax.all_gather(value_cols, "fsdp", axis=0, tiled=True),
        ),
    )
    own_ids = ctx_index * tok_rows + jnp.arange(tok_rows, dtype=jnp.int32)
    own_pos, own_seg, own_rel = stream_info(own_ids)
    query_rows = norm_rope(query_raw, q_gain, own_rel, HEAD_WIDTH)
    key_new = norm_rope(key_raw, k_gain, own_rel, HEAD_WIDTH)
    value_new = value_raw.astype(jnp.bfloat16)
    kv_heads = key_new.shape[1] // HEAD_WIDTH
    group_width = query_rows.shape[1] // key_new.shape[1]
    heads_of_query = query_rows.reshape(tok_rows, kv_heads, group_width, HEAD_WIDTH)
    pieces = (
        lax.all_gather(key_new, "ctx", axis=0, tiled=True),
        lax.all_gather(value_new, "ctx", axis=0, tiled=True),
    )
    row_ids = jnp.arange(pieces[0].shape[0], dtype=jnp.int32)
    key_pos, key_seg, unused = stream_info(row_ids)
    row_max, row_sum, weighted = sweep_keys(
        empty_state(tok_rows, kv_heads, group_width),
        heads_of_query,
        own_pos,
        own_seg,
        pieces[0],
        pieces[1],
        key_pos,
        key_seg,
    )
    attended = (weighted / row_sum[..., None]).reshape(tok_rows, -1).astype(jnp.bfloat16)
    kv_new = jnp.concatenate([key_new, value_new], axis=1)
    kv_width = kv_new.shape[1]
    per_owner = 2 * tok_rows // owner_count
    capacity = owner_count * per_owner
    own_owner = owner[0, 0]
    own_slot = slot[0, 0]
    onehot = (own_owner[:, None] == jnp.arange(owner_count, dtype=jnp.int32)[None, :]).astype(
        jnp.int32
    )
    rank_in_owner = jnp.sum(
        onehot * (jnp.cumsum(onehot, axis=0, dtype=jnp.int32) - 1), axis=1, dtype=jnp.int32
    )
    bucket_pos = own_owner * per_owner + rank_in_owner
    bucket = jnp.zeros((capacity, kv_width), jnp.bfloat16).at[bucket_pos].set(kv_new)
    bucket_slots = jnp.full((capacity,), capacity, jnp.int32).at[bucket_pos].set(own_slot)
    got_rows, got_slots = (
        lax.all_to_all(
            bucket.reshape(owner_count, per_owner, kv_width),
            ("ctx", "fsdp"),
            split_axis=0,
            concat_axis=0,
            tiled=True,
        ),
        lax.all_to_all(
            bucket_slots.reshape(owner_count, per_owner),
            ("ctx", "fsdp"),
            split_axis=0,
            concat_axis=0,
            tiled=True,
        ),
    )
    new_cache = (
        jnp.zeros((capacity, kv_width), jnp.bfloat16)
        .at[got_slots.reshape(-1)]
        .set(got_rows.reshape(-1, kv_width), mode="drop")
    )
    return (attended[None, None], new_cache)


def solution(mesh):
    placed = (
        P("ctx", "fsdp", None, None),
        P(),
        P("fsdp", "ctx"),
        P("fsdp", "ctx"),
        P("fsdp", "ctx"),
        P(),
        P(),
        P(),
        P(),
        P("ctx", "fsdp", None),
        P("ctx", "fsdp", None),
    )
    return jax.shard_map(
        shards,
        mesh=mesh,
        in_specs=placed,
        out_specs=(P("ctx", "fsdp", None, None), P(("ctx", "fsdp"), None)),
        check_vma=False,
    )
```

profile of v0, /device:TPU:1, one launch (start us, length us, event | category | flops | bytes accessed | tf_op | source)
XLA Modules:
  0.0 381.6 jit_solution(15677622843119619807)
XLA Ops:
  7.2 15.2 %all_gather.24 = bf16[128,1024]{1,0:T(8,128)(2,1)} all-gather(bf16[128,128]{1,0:T(8,128)(2,1)} %param.16), channel_id=1, replica_groups=mesh['ctx'=8,'fsdp'=16] {'ctx'}, dimensions={1}, use_global_device_ids=true | all-gather | bytes 294912 | tf_op jit(solution)/shard_map/all_gather | solution.py:156
  22.5 12.6 %all_gather.29 = bf16[128,1024]{1,0:T(8,128)(2,1)} all-gather(bf16[128,128]{1,0:T(8,128)(2,1)} %param.17), channel_id=1, replica_groups=mesh['ctx'=8,'fsdp'=16] {'ctx'}, dimensions={1}, use_global_device_ids=true | all-gather | bytes 294912 | tf_op jit(solution)/shard_map/all_gather | solution.py:157
  35.2 14.4 %all_gather.27 = bf16[128,2048]{1,0:T(8,128)(2,1)} all-gather(bf16[128,256]{1,0:T(8,128)(2,1)} %param.15), channel_id=1, replica_groups=mesh['ctx'=8,'fsdp'=16] {'ctx'}, dimensions={1}, use_global_device_ids=true | all-gather | bytes 589824 | tf_op jit(solution)/shard_map/all_gather | solution.py:155
  51.1 23.9 %all-gather.6.cloned.1.call-done = bf16[2048,1024]{1,0:T(8,128)(2,1)} async-done(((bf16[128,1024]{1,0:T(8,128)(2,1)}), bf16[2048,1024]{1,0:T(8,128)(2,1)}) %all-gather.6.cloned.1.call-update) | async-done | bytes 4194320 | tf_op jit(solution)/shard_map/all_gather | solution.py:163
  75.0 6.5 %copy.64 = bf16[1024,2048]{1,0:T(8,128)(2,1)} copy(bf16[1024,2048]{0,1:T(8,128)(2,1)} %bitcast.121) | data formatting | bytes 8388608 | tf_op jit(solution)/shard_map/dot_general | solution.py:106
  81.5 3.6 multiply_reduce_fusion.1
  85.6 1.0 copy.65
  86.7 41.8 %all-gather.12.cloned.1.call-done = bf16[2048,1024]{1,0:T(8,128)(2,1)} async-done(((bf16[128,1024]{1,0:T(8,128)(2,1)}), bf16[2048,1024]{1,0:T(8,128)(2,1)}) %all-gather.12.cloned.1.call-update) | async-done | bytes 4194320 | tf_op jit(solution)/shard_map/all_gather | solution.py:164
  128.4 4.3 %convolution_convert_fusion = bf16[256,1024]{1,0:T(8,128)(2,1)} fusion(bf16[2048,1024]{1,0:T(8,128)(2,1)} %all-gather.12.cloned.1.call-done, bf16[1,1,256,2048]{3,2,1,0:T(8,128)(2,1)S(1)} %copy-done.3, f32[2048]{0:T(1024)S(1)} %copy-done.9, f32[256]{0:T(256)S(1)} %add_rsqrt_fusion.2), kind=kOutput, calls=%fused_computation.37 | convolution fusion | flops 1076101120 | bytes 5776384 | tf_op jit(solution)/shard_map/dot_general | solution.py:106
  133.4 1.6 scatter_custom_fusion
  135.0 0.7 all_to_all.9
  135.7 7.9 %all-to-all-start = ((s32[128,1,4]{2,1,0:T(1,128)}), s32[128,1,4]{2,1,0:T(1,128)S(1)}, u32[]{:S(2)}, u32[]{:S(2)}) async-start(s32[128,1,4]{2,1,0:T(1,128)} %bitcast.26), calls=%async_computation | async-start | bytes 131072 | tf_op jit(solution)/shard_map/all_to_all | solution.py:215
  143.6 3.3 scatter_custom_fusion.1
  146.9 2.2 reshape.385
  149.1 4.1 %all-to-all-done = s32[128,1,4]{2,1,0:T(1,128)S(1)} async-done(((s32[128,1,4]{2,1,0:T(1,128)}), s32[128,1,4]{2,1,0:T(1,128)S(1)}, u32[]{:S(2)}, u32[]{:S(2)}) %all-to-all-start) | async-done | bytes 2080 | tf_op jit(solution)/shard_map/all_to_all | solution.py:215
  153.2 5.7 %all-to-all-start.1 = ((bf16[128,4,2048]{2,1,0:T(4,128)(2,1)}), bf16[128,4,2048]{2,1,0:T(4,128)(2,1)S(1)}, u32[]{:S(2)}, u32[]{:S(2)}) async-start(bf16[128,4,2048]{2,1,0:T(4,128)(2,1)} %reshape.385), calls=%async_computation.1 | async-start | bytes 4194304 | tf_op jit(solution)/shard_map/all_to_all | solution.py:208
  159.7 0.8 reduce.5
  160.7 45.7 %all-to-all-done.1 = bf16[128,4,2048]{2,1,0:T(4,128)(2,1)S(1)} async-done(((bf16[128,4,2048]{2,1,0:T(4,128)(2,1)}), bf16[128,4,2048]{2,1,0:T(4,128)(2,1)S(1)}, u32[]{:S(2)}, u32[]{:S(2)}) %all-to-all-start.1) | async-done | bytes 2097184 | tf_op jit(solution)/shard_map/all_to_all | solution.py:208
  206.4 2.1 reshape.408
  208.4 6.2 %scatter_custom_fusion.2 = bf16[512,2048]{1,0:T(8,128)(2,1)} fusion(s32[512]{0:T(512)S(1)} %bitcast.132, bf16[512,2048]{1,0:T(8,128)(2,1)} %reshape.408, bf16[]{:T(256)} %constant.129.clone.1), kind=kCustom, calls=%fused_computation.44 | custom fusion | bytes 2097664 | tf_op jit(solution)/shard_map/scatter | solution.py:226
  214.7 5.5 %all-gather.10.cloned.1.call-done = bf16[2048,2048]{1,0:T(8,128)(2,1)} async-done(((bf16[128,2048]{1,0:T(8,128)(2,1)}), bf16[2048,2048]{1,0:T(8,128)(2,1)}) %all-gather.10.cloned.1.call-update) | async-done | bytes 8388624 | tf_op jit(solution)/shard_map/all_gather | solution.py:162
  220.1 12.5 %copy.66 = bf16[2048,2048]{1,0:T(8,128)(2,1)} copy(bf16[2048,2048]{0,1:T(8,128)(2,1)} %bitcast.116) | data formatting | bytes 16777216 | tf_op jit(solution)/shard_map/dot_general | solution.py:106
  232.6 6.0 %multiply_reduce_fusion = (f32[256,16]{0,1:T(8,128)S(1)}, f32[256,16,128]{0,2,1:T(8,128)S(1)}) fusion(bf16[16,128,2048]{2,1,0:T(8,128)(2,1)} %bitcast.117, bf16[1,1,256,2048]{3,2,1,0:T(8,128)(2,1)S(1)} %copy-done.4, f32[2048]{0:T(1024)S(1)} %copy-done.9, f32[256]{0:T(256)S(1)} %add_rsqrt_fusion.2), kind=kOutput, calls=%fused_computation.36 | convolution fusion | flops 2150625280 | bytes 11559936 | tf_op jit(solution)/shard_map/dot_general | solution.py:106
  239.4 1.3 copy.68
  240.7 12.2 %all-gather.8.cloned.1.call-done = bf16[2048,1024]{1,0:T(8,128)(2,1)} async-done(((bf16[256,1024]{1,0:T(8,128)(2,1)}), bf16[2048,1024]{1,0:T(8,128)(2,1)}) %all-gather.8.cloned.1.call-update) | async-done | bytes 4194320 | tf_op jit(solution)/shard_map/all_gather | solution.py:176
  253.0 33.7 %all-gather.14.cloned.1.call-done = bf16[2048,1024]{1,0:T(8,128)(2,1)} async-done(((bf16[256,1024]{1,0:T(8,128)(2,1)}), bf16[2048,1024]{1,0:T(8,128)(2,1)}) %all-gather.14.cloned.1.call-update) | async-done | bytes 4194320 | tf_op jit(solution)/shard_map/all_gather | solution.py:177
  286.6 85.2 %while.15 = (s32[]{:T(128)}, f32[256,8,2]{0,2,1:T(2,128)S(1)}, f32[256,8,2]{0,2,1:T(2,128)S(1)}, f32[256,8,2,128]{0,3,2,1:T(8,128)}, s32[256]{0:T(256)S(1)}, /*i...) while((s32[]{:T(128)}, f32[256,8,2]{0,2,1:T(2,128)S(1)}, ...), condition=%wide.region_12.13_spmd.clone, body=%wide.region_9.12_spmd.clone.sunk | while | flops 1102991360 | bytes 41695372 | solution.py:83
  286.8 1.7 constant_dynamic-slice_fusion.8
  288.6 0.5 copy.86
  289.1 6.0 %fusion.72 = (f32[256,8,2]{0,2,1:T(2,128)S(1)}, f32[8,512,256,2]{2,1,3,0:T(8,128)}) fusion(pred[256,512]{0,1:T(8,128)(4,1)S(1)} %compare_and_fusion.2, bf16[512,8,128,1]{0,2,3,1:T(8,128)(2,1)S(1)} %bitcast.114, bf16[256,8,2,128]{3,0,2,1:T(8,128)(2,1)} %get-tuple-element.313), kind=kOutput, calls=%fused_computation.5.clone.1 | convolution fusion | flops 543158272 | bytes 10633216 | tf_op jit(solution)/shard_map/while/body/eval_jaxpr/tkgd,skd->tkgs/dot_general | solution.py:41
  295.2 4.5 %fusion.74 = f32[256,8,2]{0,2,1:T(2,128)S(1)} fusion(f32[8,512,256,2]{2,1,3,0:T(8,128)} %get-tuple-element.274, f32[256,8,2]{0,2,1:T(2,128)S(1)} %fusion.73, pred[256,512]{0,1:T(8,128)(4,1)S(1)} %compare_and_fusion.2), kind=kLoop, calls=%fused_computation.7.clone.1 | loop fusion | flops 10481664 | bytes 8552448 | tf_op jit(solution)/shard_map/while/body/eval_jaxpr/reduce_sum | solution.py:51
  299.7 0.5 copy.87
  300.2 7.2 %bitcast_add_fusion.3 = f32[256,8,2,128]{0,3,2,1:T(8,128)} fusion(f32[256,8,2,128]{0,3,2,1:T(8,128)} %get-tuple-element.294, bf16[512,8,128,1]{0,2,3,1:T(8,128)(2,1)S(1)} %bitcast.115, f32[8,512,256,2]{2,1,3,0:T(8,128)} %get-tuple-element.274, f32[256,8,2]{0,2,1:T(2,128)S(1)} %fusion.73, pred[256,512]{0,1:T(8,128)(4,1)S(1)} %compare_and_fusion.2, ...), kind=kOutput, calls=%fused_computation.10.clone.1 | convolution fusion | flops 548929536 | bytes 13795329 | tf_op jit(solution)/shard_map/while/body/eval_jaxpr/tkgs,skd->tkgd/dot_general | solution.py:52
  307.7 1.7 constant_dynamic-slice_fusion.8
  309.4 0.5 copy.86
  310.0 6.0 %fusion.72 = (f32[256,8,2]{0,2,1:T(2,128)S(1)}, f32[8,512,256,2]{2,1,3,0:T(8,128)}) fusion(pred[256,512]{0,1:T(8,128)(4,1)S(1)} %compare_and_fusion.2, bf16[512,8,128,1]{0,2,3,1:T(8,128)(2,1)S(1)} %bitcast.114, bf16[256,8,2,128]{3,0,2,1:T(8,128)(2,1)} %get-tuple-element.313), kind=kOutput, calls=%fused_computation.5.clone.1 | convolution fusion | flops 543158272 | bytes 10633216 | tf_op jit(solution)/shard_map/while/body/eval_jaxpr/tkgd,skd->tkgs/dot_general | solution.py:41
  316.0 4.5 %fusion.74 = f32[256,8,2]{0,2,1:T(2,128)S(1)} fusion(f32[8,512,256,2]{2,1,3,0:T(8,128)} %get-tuple-element.274, f32[256,8,2]{0,2,1:T(2,128)S(1)} %fusion.73, pred[256,512]{0,1:T(8,128)(4,1)S(1)} %compare_and_fusion.2), kind=kLoop, calls=%fused_computation.7.clone.1 | loop fusion | flops 10481664 | bytes 8552448 | tf_op jit(solution)/shard_map/while/body/eval_jaxpr/reduce_sum | solution.py:51
  321.1 7.8 %bitcast_add_fusion.3 = f32[256,8,2,128]{0,3,2,1:T(8,128)} fusion(f32[256,8,2,128]{0,3,2,1:T(8,128)} %get-tuple-element.294, bf16[512,8,128,1]{0,2,3,1:T(8,128)(2,1)S(1)} %bitcast.115, f32[8,512,256,2]{2,1,3,0:T(8,128)} %get-tuple-element.274, f32[256,8,2]{0,2,1:T(2,128)S(1)} %fusion.73, pred[256,512]{0,1:T(8,128)(4,1)S(1)} %compare_and_fusion.2, ...), kind=kOutput, calls=%fused_computation.10.clone.1 | convolution fusion | flops 548929536 | bytes 13795329 | tf_op jit(solution)/shard_map/while/body/eval_jaxpr/tkgs,skd->tkgd/dot_general | solution.py:52
  329.1 1.7 constant_dynamic-slice_fusion.8
  331.4 6.0 %fusion.72 = (f32[256,8,2]{0,2,1:T(2,128)S(1)}, f32[8,512,256,2]{2,1,3,0:T(8,128)}) fusion(pred[256,512]{0,1:T(8,128)(4,1)S(1)} %compare_and_fusion.2, bf16[512,8,128,1]{0,2,3,1:T(8,128)(2,1)S(1)} %bitcast.114, bf16[256,8,2,128]{3,0,2,1:T(8,128)(2,1)} %get-tuple-element.313), kind=kOutput, calls=%fused_computation.5.clone.1 | convolution fusion | flops 543158272 | bytes 10633216 | tf_op jit(solution)/shard_map/while/body/eval_jaxpr/tkgd,skd->tkgs/dot_general | solution.py:41
  337.5 4.5 %fusion.74 = f32[256,8,2]{0,2,1:T(2,128)S(1)} fusion(f32[8,512,256,2]{2,1,3,0:T(8,128)} %get-tuple-element.274, f32[256,8,2]{0,2,1:T(2,128)S(1)} %fusion.73, pred[256,512]{0,1:T(8,128)(4,1)S(1)} %compare_and_fusion.2), kind=kLoop, calls=%fused_computation.7.clone.1 | loop fusion | flops 10481664 | bytes 8552448 | tf_op jit(solution)/shard_map/while/body/eval_jaxpr/reduce_sum | solution.py:51
  342.5 7.8 %bitcast_add_fusion.3 = f32[256,8,2,128]{0,3,2,1:T(8,128)} fusion(f32[256,8,2,128]{0,3,2,1:T(8,128)} %get-tuple-element.294, bf16[512,8,128,1]{0,2,3,1:T(8,128)(2,1)S(1)} %bitcast.115, f32[8,512,256,2]{2,1,3,0:T(8,128)} %get-tuple-element.274, f32[256,8,2]{0,2,1:T(2,128)S(1)} %fusion.73, pred[256,512]{0,1:T(8,128)(4,1)S(1)} %compare_and_fusion.2, ...), kind=kOutput, calls=%fused_computation.10.clone.1 | convolution fusion | flops 548929536 | bytes 13795329 | tf_op jit(solution)/shard_map/while/body/eval_jaxpr/tkgs,skd->tkgd/dot_general | solution.py:52
  350.6 1.7 constant_dynamic-slice_fusion.8
  352.9 6.0 %fusion.72 = (f32[256,8,2]{0,2,1:T(2,128)S(1)}, f32[8,512,256,2]{2,1,3,0:T(8,128)}) fusion(pred[256,512]{0,1:T(8,128)(4,1)S(1)} %compare_and_fusion.2, bf16[512,8,128,1]{0,2,3,1:T(8,128)(2,1)S(1)} %bitcast.114, bf16[256,8,2,128]{3,0,2,1:T(8,128)(2,1)} %get-tuple-element.313), kind=kOutput, calls=%fused_computation.5.clone.1 | convolution fusion | flops 543158272 | bytes 10633216 | tf_op jit(solution)/shard_map/while/body/eval_jaxpr/tkgd,skd->tkgs/dot_general | solution.py:41
  358.9 4.5 %fusion.74 = f32[256,8,2]{0,2,1:T(2,128)S(1)} fusion(f32[8,512,256,2]{2,1,3,0:T(8,128)} %get-tuple-element.274, f32[256,8,2]{0,2,1:T(2,128)S(1)} %fusion.73, pred[256,512]{0,1:T(8,128)(4,1)S(1)} %compare_and_fusion.2), kind=kLoop, calls=%fused_computation.7.clone.1 | loop fusion | flops 10481664 | bytes 8552448 | tf_op jit(solution)/shard_map/while/body/eval_jaxpr/reduce_sum | solution.py:51
  364.0 7.8 %bitcast_add_fusion.3 = f32[256,8,2,128]{0,3,2,1:T(8,128)} fusion(f32[256,8,2,128]{0,3,2,1:T(8,128)} %get-tuple-element.294, bf16[512,8,128,1]{0,2,3,1:T(8,128)(2,1)S(1)} %bitcast.115, f32[8,512,256,2]{2,1,3,0:T(8,128)} %get-tuple-element.274, f32[256,8,2]{0,2,1:T(2,128)S(1)} %fusion.73, pred[256,512]{0,1:T(8,128)(4,1)S(1)} %compare_and_fusion.2, ...), kind=kOutput, calls=%fused_computation.10.clone.1 | convolution fusion | flops 548929536 | bytes 13795329 | tf_op jit(solution)/shard_map/while/body/eval_jaxpr/tkgs,skd->tkgd/dot_general | solution.py:52
  371.8 1.8 divide_convert_fusion
  373.6 1.4 copy.78
  (100 shorter events, 8.2 us)
Async XLA Ops:
  7.2 42.5 %copy-start = (s32[16,8]{0,1:T(8,128)S(1)}, s32[16,8]{0,1:T(8,128)}, u32[]{:S(2)}) copy-start(s32[16,8]{0,1:T(8,128)} %param.21) | copy-start | bytes 1540
  7.2 42.7 %copy-start.6 = (s32[16,4]{0,1:T(4,128)S(1)}, s32[16,4]{0,1:T(4,128)}, u32[]{:S(2)}) copy-start(s32[16,4]{0,1:T(4,128)} %param.20) | copy-start | bytes 772
  7.2 43.3 %copy-start.3 = (bf16[1,1,256,2048]{3,2,1,0:T(8,128)(2,1)S(1)}, bf16[1,1,256,2048]{3,2,1,0:T(8,128)(2,1)}, u32[]{:S(2)}) copy-start(bf16[1,1,256,2048]{3,2,1,0:T(8,128)(2,1)} %param.13) | copy-start | bytes 3145732
  7.2 67.8 %all-gather.6.cloned.1.call-start = ((), (), s32[]{:S(2)}) async-start(), calls=%async_computation.2 | async-start | bytes 4456448 | tf_op jit(solution)/shard_map/all_gather | solution.py:163
  22.5 106.0 %all-gather.12.cloned.1.call-start = ((), (), s32[]{:S(2)}) async-start(), calls=%async_computation.5 | async-start | bytes 4456448 | tf_op jit(solution)/shard_map/all_gather | solution.py:164
  35.1 185.0 %all-gather.10.cloned.1.call-start = ((), (), s32[]{:S(2)}) async-start(), calls=%async_computation.4 | async-start | bytes 8912896 | tf_op jit(solution)/shard_map/all_gather | solution.py:162
  49.6 203.4 %all-gather.8.cloned.1.call-start = ((), (), s32[]{:S(2)}) async-start(), calls=%async_computation.3 | async-start | bytes 4718592 | tf_op jit(solution)/shard_map/all_gather | solution.py:176
  75.0 6.5 %copy-start.9 = (f32[2048]{0:T(1024)S(1)}, f32[2048]{0:T(1024)}, u32[]{:S(2)}) copy-start(f32[2048]{0:T(1024)} %param.14) | copy-start | bytes 24580
  81.5 3.6 copy-start.7
  86.6 46.1 %copy-start.5 = (s32[1,1,256]{2,1,0:T(1,128)S(1)}, s32[1,1,256]{2,1,0:T(1,128)}, u32[]{:S(2)}) copy-start(s32[1,1,256]{2,1,0:T(1,128)} %param.22) | copy-start | bytes 3076
  86.6 57.0 %copy-start.2 = (bf16[256,1024]{1,0:T(8,128)(2,1)S(1)}, bf16[256,1024]{1,0:T(8,128)(2,1)}, u32[]{:S(2)}) copy-start(bf16[256,1024]{1,0:T(8,128)(2,1)} %copy.65) | copy-start | bytes 1572868
  86.6 200.0 %all-gather.14.cloned.1.call-start = ((), (), s32[]{:S(2)}) async-start(), calls=%async_computation.6 | async-start | bytes 4718592 | tf_op jit(solution)/shard_map/all_gather | solution.py:177
  135.7 17.5 %all-to-all-start = ((s32[128,1,4]{2,1,0:T(1,128)}), s32[128,1,4]{2,1,0:T(1,128)S(1)}, u32[]{:S(2)}, u32[]{:S(2)}) async-start(s32[128,1,4]{2,1,0:T(1,128)} %bitcast.26), calls=%async_computation | async-start | bytes 131072 | tf_op jit(solution)/shard_map/all_to_all | solution.py:215
  153.2 53.2 %all-to-all-start.1 = ((bf16[128,4,2048]{2,1,0:T(4,128)(2,1)}), bf16[128,4,2048]{2,1,0:T(4,128)(2,1)S(1)}, u32[]{:S(2)}, u32[]{:S(2)}) async-start(bf16[128,4,2048]{2,1,0:T(4,128)(2,1)} %reshape.385), calls=%async_computation.1 | async-start | bytes 4194304 | tf_op jit(solution)/shard_map/all_to_all | solution.py:208
  220.1 12.5 %copy-start.4 = (bf16[1,1,256,2048]{3,2,1,0:T(8,128)(2,1)S(1)}, bf16[1,1,256,2048]{3,2,1,0:T(8,128)(2,1)}, u32[]{:S(2)}) copy-start(bf16[1,1,256,2048]{3,2,1,0:T(8,128)(2,1)} %param.13) | copy-start | bytes 3145732
  232.6 6.0 %copy-start.8 = (f32[128]{0:T(128)S(1)}, f32[128]{0:T(128)}, u32[]{:S(2)}) copy-start(f32[128]{0:T(128)} %param.18) | copy-start | bytes 1540
  371.8 3.2 copy-start.1
Sparse Core Ops, SparseCore 0:
  22.6 52.4 all-gather.5
  77.2 51.2 all-gather.11
  130.6 89.4 all-gather.9
  221.7 31.2 all-gather.7
  254.5 32.0 all-gather.13
where the time goes:
time: 383 us; the launch traced here: 382 us
  waiting for transfers between devices  167 us (44%)
  matrix products  68.6 us (18%)
  local copies, waits for them, and re-layouts  48 us (13%)
  blocking collectives  42.2 us (11%)
  other arithmetic  27.9 us (7%)
  between operations  14.1 us (4%)
  starting transfers between devices  13.8 us (4%)
    all_to_all x1, waiting for transfers between devices, shards(): lax.all_to_all(bucket.reshape(owner_count, per_owner, kv_width), ('ctx',...  45.7 us
    all_gather x1, waiting for transfers between devices, shards(): lax.all_gather(value_cols, 'fsdp', axis=0, tiled=True)  41.8 us
    all_gather x1, waiting for transfers between devices, shards(): lax.all_gather(value_new, 'ctx', axis=0, tiled=True)  33.7 us
    dot_general x4, matrix products, attend_keys(): jnp.einsum('tkgs,skd->tkgd', weights.astype(jnp.bfloat16), heads_of_value...  30.7 us
    dot_general x4, matrix products, attend_keys(): jnp.einsum('tkgd,skd->tkgs', heads_of_query, heads_of_key, preferred_elem...  24.1 us
    all_gather x1, waiting for transfers between devices, shards(): lax.all_gather(key_cols, 'fsdp', axis=0, tiled=True)  23.9 us
    dot_general x2, local copies, waits for them, and re-layouts, project_rows(): jnp.dot(source, shard_rows, preferred_element_type=jnp.float32)  19 us
    reduce_sum x4, other arithmetic, attend_keys(): row_sum = row_sum * shrink + jnp.sum(weights, axis=-1)  17.9 us
  transfers between devices with their start and end apart: 7, of which 7 were waited for; matrix products, arithmetic and copies ran while one was open for 15% of the time, Pallas kernels for 0%

commit v1 on v0

--- a/solution.py
+++ b/solution.py
@@ -152,7 +152,9 @@
         return (positions, segment, relative)
 
     query_cols, key_cols, value_cols = (
-        lax.all_gather(w_query, "ctx", axis=1, tiled=True),
+        jnp.concatenate(
+            lax.all_to_all(jnp.stack([w_query] * lax.axis_size("ctx")), "ctx", 0, 0), axis=1
+        ),
         lax.all_gather(w_key, "ctx", axis=1, tiled=True),
         lax.all_gather(w_value, "ctx", axis=1, tiled=True),
     )

time: 383 us -> 387 us (1.010)
  waiting for transfers between devices: 167 us -> 184 us
  local copies, waits for them, and re-layouts: 48 us -> 36.4 us
    all_gather x1 -> x0, blocking collectives: 14.4 us -> none  [shards(): lax.all_gather(w_query, 'ctx', axis=1, tiled=True)]
    all_gather x1, waiting for transfers between devices: 12.2 us -> 26 us  [shards(): lax.all_gather(key_new, 'ctx', axis=0, tiled=True)]
    all_to_all x0 -> x1, blocking collectives: none -> 13.4 us  [shards(): lax.all_to_all(jnp.stack([w_query] * lax.axis_size('ctx')), 'ctx', 0, 0)]
    dot_general x2 -> x1, local copies, waits for them, and re-layouts: 19 us -> 6.5 us  [project_rows(): jnp.dot(source, shard_rows, preferred_element_type=jnp.float32)]
    all_gather x1, waiting for transfers between devices: 5.47 us -> 15.7 us  [shards(): lax.all_gather(query_cols, 'fsdp', axis=0, tiled=True)]
    all_to_all x1, waiting for transfers between devices: 45.7 us -> 39.2 us  [shards(): lax.all_to_all(bucket.reshape(owner_count, per_owner, kv_width), ('ctx',...]
  transfers between devices with their start and end apart: 7 -> 7, of which waited for: 7 -> 7; matrix products, arithmetic and copies ran while one was open for 15% -> 11% of each run, Pallas kernels for 0% -> 0%
where the time goes in v1:
time: 387 us; the launch traced here: 386 us
  waiting for transfers between devices  184 us (48%)
  matrix products  68.5 us (18%)
  blocking collectives  41.1 us (11%)
  local copies, waits for them, and re-layouts  36.4 us (9%)
  other arithmetic  27.9 us (7%)
  between operations  14.1 us (4%)
  starting transfers between devices  13.9 us (4%)
    all_gather x1, waiting for transfers between devices, shards(): lax.all_gather(value_cols, 'fsdp', axis=0, tiled=True)  41.8 us
    all_to_all x1, waiting for transfers between devices, shards(): lax.all_to_all(bucket.reshape(owner_count, per_owner, kv_width), ('ctx',...  39.2 us
    all_gather x1, waiting for transfers between devices, shards(): lax.all_gather(value_new, 'ctx', axis=0, tiled=True)  33.7 us
    dot_general x4, matrix products, attend_keys(): jnp.einsum('tkgs,skd->tkgd', weights.astype(jnp.bfloat16), heads_of_value...  30.5 us
    all_gather x1, waiting for transfers between devices, shards(): lax.all_gather(key_new, 'ctx', axis=0, tiled=True)  26 us
    dot_general x4, matrix products, attend_keys(): jnp.einsum('tkgd,skd->tkgs', heads_of_query, heads_of_key, preferred_elem...  24.1 us
    all_gather x1, waiting for transfers between devices, shards(): lax.all_gather(key_cols, 'fsdp', axis=0, tiled=True)  23.9 us
    reduce_sum x4, other arithmetic, attend_keys(): row_sum = row_sum * shrink + jnp.sum(weights, axis=-1)  17.9 us
  transfers between devices with their start and end apart: 7, of which 7 were waited for; matrix products, arithmetic and copies ran while one was open for 11% of the time, Pallas kernels for 0%

profile of v1, /device:TPU:1, one launch (start us, length us, event | category | flops | bytes accessed | tf_op | source)
XLA Modules:
  0.0 386.4 jit_solution(12697123467241126561)
XLA Ops:
  7.2 15.2 %all_gather.21 = bf16[128,1024]{1,0:T(8,128)(2,1)} all-gather(bf16[128,128]{1,0:T(8,128)(2,1)} %param.16), channel_id=1, replica_groups=mesh['ctx'=8,'fsdp'=16] {'ctx'}, dimensions={1}, use_global_device_ids=true | all-gather | bytes 294912 | tf_op jit(solution)/shard_map/all_gather | solution.py:158
  22.5 12.6 %all_gather.25 = bf16[128,1024]{1,0:T(8,128)(2,1)} all-gather(bf16[128,128]{1,0:T(8,128)(2,1)} %param.17), channel_id=1, replica_groups=mesh['ctx'=8,'fsdp'=16] {'ctx'}, dimensions={1}, use_global_device_ids=true | all-gather | bytes 294912 | tf_op jit(solution)/shard_map/all_gather | solution.py:159
  35.2 1.0 copy.66
  36.2 13.4 %all_to_all.19 = bf16[8,128,256]{1,2,0:T(8,128)(2,1)} all-to-all(bf16[8,128,256]{1,2,0:T(8,128)(2,1)S(1)} %stack.2), channel_id=1, replica_groups=mesh['ctx'=8,'fsdp'=16] {'ctx'}, dimensions={0} | all-to-all | bytes 1048576 | tf_op jit(solution)/shard_map/all_to_all | solution.py:156
  51.1 23.9 %all-gather.6.cloned.1.call-done = bf16[2048,1024]{1,0:T(8,128)(2,1)} async-done(((bf16[128,1024]{1,0:T(8,128)(2,1)}), bf16[2048,1024]{1,0:T(8,128)(2,1)}) %all-gather.6.cloned.1.call-update) | async-done | bytes 4194320 | tf_op jit(solution)/shard_map/all_gather | solution.py:165
  75.0 6.5 %copy.64 = bf16[1024,2048]{1,0:T(8,128)(2,1)} copy(bf16[1024,2048]{0,1:T(8,128)(2,1)} %bitcast.123) | data formatting | bytes 8388608 | tf_op jit(solution)/shard_map/dot_general | solution.py:106
  81.5 3.6 multiply_reduce_fusion.1
  85.6 1.0 copy.65
  86.7 41.8 %all-gather.12.cloned.1.call-done = bf16[2048,1024]{1,0:T(8,128)(2,1)} async-done(((bf16[128,1024]{1,0:T(8,128)(2,1)}), bf16[2048,1024]{1,0:T(8,128)(2,1)}) %all-gather.12.cloned.1.call-update) | async-done | bytes 4194320 | tf_op jit(solution)/shard_map/all_gather | solution.py:166
  128.4 4.3 %convolution_convert_fusion = bf16[256,1024]{1,0:T(8,128)(2,1)} fusion(bf16[2048,1024]{1,0:T(8,128)(2,1)} %all-gather.12.cloned.1.call-done, bf16[1,1,256,2048]{3,2,1,0:T(8,128)(2,1)S(1)} %copy-done.3, f32[2048]{0:T(1024)S(1)} %copy-done.9, f32[256]{0:T(256)S(1)} %add_rsqrt_fusion.2), kind=kOutput, calls=%fused_computation.37 | convolution fusion | flops 1076101120 | bytes 5776384 | tf_op jit(solution)/shard_map/dot_general | solution.py:106
  133.4 1.6 scatter_custom_fusion
  135.0 0.7 all_to_all.13
  135.7 7.9 %all-to-all-start.1 = ((s32[128,1,4]{2,1,0:T(1,128)}), s32[128,1,4]{2,1,0:T(1,128)S(1)}, u32[]{:S(2)}, u32[]{:S(2)}) async-start(s32[128,1,4]{2,1,0:T(1,128)} %bitcast.28), calls=%async_computation.1 | async-start | bytes 131072 | tf_op jit(solution)/shard_map/all_to_all | solution.py:217
  143.6 3.3 scatter_custom_fusion.1
  146.9 2.2 reshape.395
  149.2 3.9 %all-to-all-done.1 = s32[128,1,4]{2,1,0:T(1,128)S(1)} async-done(((s32[128,1,4]{2,1,0:T(1,128)}), s32[128,1,4]{2,1,0:T(1,128)S(1)}, u32[]{:S(2)}, u32[]{:S(2)}) %all-to-all-start.1) | async-done | bytes 2080 | tf_op jit(solution)/shard_map/all_to_all | solution.py:217
  153.1 5.9 %all-to-all-start.2 = ((bf16[128,4,2048]{2,1,0:T(4,128)(2,1)}), bf16[128,4,2048]{2,1,0:T(4,128)(2,1)S(1)}, u32[]{:S(2)}, u32[]{:S(2)}) async-start(bf16[128,4,2048]{2,1,0:T(4,128)(2,1)} %reshape.395), calls=%async_computation.2 | async-start | bytes 4194304 | tf_op jit(solution)/shard_map/all_to_all | solution.py:210
  159.7 0.8 reduce.5
  160.7 39.2 %all-to-all-done.2 = bf16[128,4,2048]{2,1,0:T(4,128)(2,1)S(1)} async-done(((bf16[128,4,2048]{2,1,0:T(4,128)(2,1)}), bf16[128,4,2048]{2,1,0:T(4,128)(2,1)S(1)}, u32[]{:S(2)}, u32[]{:S(2)}) %all-to-all-start.2) | async-done | bytes 2097184 | tf_op jit(solution)/shard_map/all_to_all | solution.py:210
  199.8 2.0 reshape.418
  201.9 6.2 %scatter_custom_fusion.2 = bf16[512,2048]{1,0:T(8,128)(2,1)} fusion(s32[512]{0:T(512)S(1)} %bitcast.135, bf16[512,2048]{1,0:T(8,128)(2,1)} %reshape.418, bf16[]{:T(256)} %constant.129.clone.1), kind=kCustom, calls=%fused_computation.44 | custom fusion | bytes 2097664 | tf_op jit(solution)/shard_map/scatter | solution.py:228
  208.1 15.7 %all-gather.10.cloned.1.call-done = bf16[2048,2048]{0,1:T(8,128)(2,1)} async-done(((bf16[128,2048]{0,1:T(8,128)(2,1)}), bf16[2048,2048]{0,1:T(8,128)(2,1)}) %all-gather.10.cloned.1.call-update) | async-done | bytes 8388624 | tf_op jit(solution)/shard_map/all_gather | solution.py:164
  223.8 6.0 %multiply_reduce_fusion = (f32[256,16]{0,1:T(8,128)S(1)}, f32[256,16,128]{0,2,1:T(8,128)S(1)}) fusion(bf16[16,128,2048]{2,1,0:T(8,128)(2,1)} %bitcast.139, bf16[1,1,256,2048]{3,2,1,0:T(8,128)(2,1)S(1)} %copy-done.4, f32[2048]{0:T(1024)S(1)} %copy-done.9, f32[256]{0:T(256)S(1)} %add_rsqrt_fusion.2), kind=kOutput, calls=%fused_computation.36 | convolution fusion | flops 2150625280 | bytes 11559936 | tf_op jit(solution)/shard_map/dot_general | solution.py:106
  230.6 1.3 copy.68
  231.9 26.0 %all-gather.8.cloned.1.call-done = bf16[2048,1024]{1,0:T(8,128)(2,1)} async-done(((bf16[256,1024]{1,0:T(8,128)(2,1)}), bf16[2048,1024]{1,0:T(8,128)(2,1)}) %all-gather.8.cloned.1.call-update) | async-done | bytes 4194320 | tf_op jit(solution)/shard_map/all_gather | solution.py:178
  257.9 33.7 %all-gather.14.cloned.1.call-done = bf16[2048,1024]{1,0:T(8,128)(2,1)} async-done(((bf16[256,1024]{1,0:T(8,128)(2,1)}), bf16[2048,1024]{1,0:T(8,128)(2,1)}) %all-gather.14.cloned.1.call-update) | async-done | bytes 4194320 | tf_op jit(solution)/shard_map/all_gather | solution.py:179
  291.6 85.0 %while.15 = (s32[]{:T(128)}, f32[256,8,2]{0,2,1:T(2,128)S(1)}, f32[256,8,2]{0,2,1:T(2,128)S(1)}, f32[256,8,2,128]{0,3,2,1:T(8,128)}, s32[256]{0:T(256)S(1)}, /*i...) while((s32[]{:T(128)}, f32[256,8,2]{0,2,1:T(2,128)S(1)}, ...), condition=%wide.region_12.13_spmd.clone, body=%wide.region_9.12_spmd.clone.sunk | while | flops 1102991360 | bytes 41695372 | solution.py:83
  291.8 1.7 constant_dynamic-slice_fusion.8
  293.5 0.5 copy.86
  294.1 6.0 %fusion.72 = (f32[256,8,2]{0,2,1:T(2,128)S(1)}, f32[8,512,256,2]{2,1,3,0:T(8,128)}) fusion(pred[256,512]{0,1:T(8,128)(4,1)S(1)} %compare_and_fusion.2, bf16[512,8,128,1]{0,2,3,1:T(8,128)(2,1)S(1)} %bitcast.118, bf16[256,8,2,128]{3,0,2,1:T(8,128)(2,1)} %get-tuple-element.313), kind=kOutput, calls=%fused_computation.5.clone.1 | convolution fusion | flops 543158272 | bytes 10633216 | tf_op jit(solution)/shard_map/while/body/eval_jaxpr/tkgd,skd->tkgs/dot_general | solution.py:41
  300.1 4.5 %fusion.74 = f32[256,8,2]{0,2,1:T(2,128)S(1)} fusion(f32[8,512,256,2]{2,1,3,0:T(8,128)} %get-tuple-element.274, f32[256,8,2]{0,2,1:T(2,128)S(1)} %fusion.73, pred[256,512]{0,1:T(8,128)(4,1)S(1)} %compare_and_fusion.2), kind=kLoop, calls=%fused_computation.7.clone.1 | loop fusion | flops 10481664 | bytes 8552448 | tf_op jit(solution)/shard_map/while/body/eval_jaxpr/reduce_sum | solution.py:51
  304.6 0.5 copy.87
  305.2 7.2 %bitcast_add_fusion.3 = f32[256,8,2,128]{0,3,2,1:T(8,128)} fusion(f32[256,8,2,128]{0,3,2,1:T(8,128)} %get-tuple-element.294, bf16[512,8,128,1]{0,2,3,1:T(8,128)(2,1)S(1)} %bitcast.119, f32[8,512,256,2]{2,1,3,0:T(8,128)} %get-tuple-element.274, f32[256,8,2]{0,2,1:T(2,128)S(1)} %fusion.73, pred[256,512]{0,1:T(8,128)(4,1)S(1)} %compare_and_fusion.2, ...), kind=kOutput, calls=%fused_computation.10.clone.1 | convolution fusion | flops 548929536 | bytes 13795329 | tf_op jit(solution)/shard_map/while/body/eval_jaxpr/tkgs,skd->tkgd/dot_general | solution.py:52
  312.6 1.7 constant_dynamic-slice_fusion.8
  314.9 6.0 %fusion.72 = (f32[256,8,2]{0,2,1:T(2,128)S(1)}, f32[8,512,256,2]{2,1,3,0:T(8,128)}) fusion(pred[256,512]{0,1:T(8,128)(4,1)S(1)} %compare_and_fusion.2, bf16[512,8,128,1]{0,2,3,1:T(8,128)(2,1)S(1)} %bitcast.118, bf16[256,8,2,128]{3,0,2,1:T(8,128)(2,1)} %get-tuple-element.313), kind=kOutput, calls=%fused_computation.5.clone.1 | convolution fusion | flops 543158272 | bytes 10633216 | tf_op jit(solution)/shard_map/while/body/eval_jaxpr/tkgd,skd->tkgs/dot_general | solution.py:41
  320.9 4.5 %fusion.74 = f32[256,8,2]{0,2,1:T(2,128)S(1)} fusion(f32[8,512,256,2]{2,1,3,0:T(8,128)} %get-tuple-element.274, f32[256,8,2]{0,2,1:T(2,128)S(1)} %fusion.73, pred[256,512]{0,1:T(8,128)(4,1)S(1)} %compare_and_fusion.2), kind=kLoop, calls=%fused_computation.7.clone.1 | loop fusion | flops 10481664 | bytes 8552448 | tf_op jit(solution)/shard_map/while/body/eval_jaxpr/reduce_sum | solution.py:51
  326.0 7.8 %bitcast_add_fusion.3 = f32[256,8,2,128]{0,3,2,1:T(8,128)} fusion(f32[256,8,2,128]{0,3,2,1:T(8,128)} %get-tuple-element.294, bf16[512,8,128,1]{0,2,3,1:T(8,128)(2,1)S(1)} %bitcast.119, f32[8,512,256,2]{2,1,3,0:T(8,128)} %get-tuple-element.274, f32[256,8,2]{0,2,1:T(2,128)S(1)} %fusion.73, pred[256,512]{0,1:T(8,128)(4,1)S(1)} %compare_and_fusion.2, ...), kind=kOutput, calls=%fused_computation.10.clone.1 | convolution fusion | flops 548929536 | bytes 13795329 | tf_op jit(solution)/shard_map/while/body/eval_jaxpr/tkgs,skd->tkgd/dot_general | solution.py:52
  334.0 1.7 constant_dynamic-slice_fusion.8
  336.3 6.0 %fusion.72 = (f32[256,8,2]{0,2,1:T(2,128)S(1)}, f32[8,512,256,2]{2,1,3,0:T(8,128)}) fusion(pred[256,512]{0,1:T(8,128)(4,1)S(1)} %compare_and_fusion.2, bf16[512,8,128,1]{0,2,3,1:T(8,128)(2,1)S(1)} %bitcast.118, bf16[256,8,2,128]{3,0,2,1:T(8,128)(2,1)} %get-tuple-element.313), kind=kOutput, calls=%fused_computation.5.clone.1 | convolution fusion | flops 543158272 | bytes 10633216 | tf_op jit(solution)/shard_map/while/body/eval_jaxpr/tkgd,skd->tkgs/dot_general | solution.py:41
  342.3 4.5 %fusion.74 = f32[256,8,2]{0,2,1:T(2,128)S(1)} fusion(f32[8,512,256,2]{2,1,3,0:T(8,128)} %get-tuple-element.274, f32[256,8,2]{0,2,1:T(2,128)S(1)} %fusion.73, pred[256,512]{0,1:T(8,128)(4,1)S(1)} %compare_and_fusion.2), kind=kLoop, calls=%fused_computation.7.clone.1 | loop fusion | flops 10481664 | bytes 8552448 | tf_op jit(solution)/shard_map/while/body/eval_jaxpr/reduce_sum | solution.py:51
  347.4 7.8 %bitcast_add_fusion.3 = f32[256,8,2,128]{0,3,2,1:T(8,128)} fusion(f32[256,8,2,128]{0,3,2,1:T(8,128)} %get-tuple-element.294, bf16[512,8,128,1]{0,2,3,1:T(8,128)(2,1)S(1)} %bitcast.119, f32[8,512,256,2]{2,1,3,0:T(8,128)} %get-tuple-element.274, f32[256,8,2]{0,2,1:T(2,128)S(1)} %fusion.73, pred[256,512]{0,1:T(8,128)(4,1)S(1)} %compare_and_fusion.2, ...), kind=kOutput, calls=%fused_computation.10.clone.1 | convolution fusion | flops 548929536 | bytes 13795329 | tf_op jit(solution)/shard_map/while/body/eval_jaxpr/tkgs,skd->tkgd/dot_general | solution.py:52
  355.4 1.7 constant_dynamic-slice_fusion.8
  357.7 6.0 %fusion.72 = (f32[256,8,2]{0,2,1:T(2,128)S(1)}, f32[8,512,256,2]{2,1,3,0:T(8,128)}) fusion(pred[256,512]{0,1:T(8,128)(4,1)S(1)} %compare_and_fusion.2, bf16[512,8,128,1]{0,2,3,1:T(8,128)(2,1)S(1)} %bitcast.118, bf16[256,8,2,128]{3,0,2,1:T(8,128)(2,1)} %get-tuple-element.313), kind=kOutput, calls=%fused_computation.5.clone.1 | convolution fusion | flops 543158272 | bytes 10633216 | tf_op jit(solution)/shard_map/while/body/eval_jaxpr/tkgd,skd->tkgs/dot_general | solution.py:41
  363.7 4.5 %fusion.74 = f32[256,8,2]{0,2,1:T(2,128)S(1)} fusion(f32[8,512,256,2]{2,1,3,0:T(8,128)} %get-tuple-element.274, f32[256,8,2]{0,2,1:T(2,128)S(1)} %fusion.73, pred[256,512]{0,1:T(8,128)(4,1)S(1)} %compare_and_fusion.2), kind=kLoop, calls=%fused_computation.7.clone.1 | loop fusion | flops 10481664 | bytes 8552448 | tf_op jit(solution)/shard_map/while/body/eval_jaxpr/reduce_sum | solution.py:51
  368.3 0.5 copy.87
  368.8 7.8 %bitcast_add_fusion.3 = f32[256,8,2,128]{0,3,2,1:T(8,128)} fusion(f32[256,8,2,128]{0,3,2,1:T(8,128)} %get-tuple-element.294, bf16[512,8,128,1]{0,2,3,1:T(8,128)(2,1)S(1)} %bitcast.119, f32[8,512,256,2]{2,1,3,0:T(8,128)} %get-tuple-element.274, f32[256,8,2]{0,2,1:T(2,128)S(1)} %fusion.73, pred[256,512]{0,1:T(8,128)(4,1)S(1)} %compare_and_fusion.2, ...), kind=kOutput, calls=%fused_computation.10.clone.1 | convolution fusion | flops 548929536 | bytes 13795329 | tf_op jit(solution)/shard_map/while/body/eval_jaxpr/tkgs,skd->tkgd/dot_general | solution.py:52
  376.6 1.8 divide_convert_fusion
  378.4 1.4 copy.78
  (101 shorter events, 8.3 us)
Async XLA Ops:
  7.2 42.5 %copy-start = (s32[16,8]{0,1:T(8,128)S(1)}, s32[16,8]{0,1:T(8,128)}, u32[]{:S(2)}) copy-start(s32[16,8]{0,1:T(8,128)} %param.21) | copy-start | bytes 1540
  7.2 42.7 %copy-start.6 = (s32[16,4]{0,1:T(4,128)S(1)}, s32[16,4]{0,1:T(4,128)}, u32[]{:S(2)}) copy-start(s32[16,4]{0,1:T(4,128)} %param.20) | copy-start | bytes 772
  7.2 43.3 %copy-start.3 = (bf16[1,1,256,2048]{3,2,1,0:T(8,128)(2,1)S(1)}, bf16[1,1,256,2048]{3,2,1,0:T(8,128)(2,1)}, u32[]{:S(2)}) copy-start(bf16[1,1,256,2048]{3,2,1,0:T(8,128)(2,1)} %param.13) | copy-start | bytes 3145732
  7.2 67.8 %all-gather.6.cloned.1.call-start = ((), (), s32[]{:S(2)}) async-start(), calls=%async_computation.3 | async-start | bytes 4456448 | tf_op jit(solution)/shard_map/all_gather | solution.py:165
  22.5 106.0 %all-gather.12.cloned.1.call-start = ((), (), s32[]{:S(2)}) async-start(), calls=%async_computation.6 | async-start | bytes 4456448 | tf_op jit(solution)/shard_map/all_gather | solution.py:166
  35.1 188.7 %all-gather.10.cloned.1.call-start = ((), (), s32[]{:S(2)}) async-start(), calls=%async_computation.5 | async-start | bytes 8912896 | tf_op jit(solution)/shard_map/all_gather | solution.py:164
  49.6 208.3 %all-gather.8.cloned.1.call-start = ((), (), s32[]{:S(2)}) async-start(), calls=%async_computation.4 | async-start | bytes 4718592 | tf_op jit(solution)/shard_map/all_gather | solution.py:178
  75.0 6.5 %copy-start.9 = (f32[2048]{0:T(1024)S(1)}, f32[2048]{0:T(1024)}, u32[]{:S(2)}) copy-start(f32[2048]{0:T(1024)} %param.14) | copy-start | bytes 24580
  81.5 3.6 copy-start.7
  86.6 46.2 %copy-start.5 = (s32[1,1,256]{2,1,0:T(1,128)S(1)}, s32[1,1,256]{2,1,0:T(1,128)}, u32[]{:S(2)}) copy-start(s32[1,1,256]{2,1,0:T(1,128)} %param.22) | copy-start | bytes 3076
  86.6 57.0 %copy-start.2 = (bf16[256,1024]{1,0:T(8,128)(2,1)S(1)}, bf16[256,1024]{1,0:T(8,128)(2,1)}, u32[]{:S(2)}) copy-start(bf16[256,1024]{1,0:T(8,128)(2,1)} %copy.65) | copy-start | bytes 1572868
  86.6 204.9 %all-gather.14.cloned.1.call-start = ((), (), s32[]{:S(2)}) async-start(), calls=%async_computation.7 | async-start | bytes 4718592 | tf_op jit(solution)/shard_map/all_gather | solution.py:179
  135.7 17.3 %all-to-all-start.1 = ((s32[128,1,4]{2,1,0:T(1,128)}), s32[128,1,4]{2,1,0:T(1,128)S(1)}, u32[]{:S(2)}, u32[]{:S(2)}) async-start(s32[128,1,4]{2,1,0:T(1,128)} %bitcast.28), calls=%async_computation.1 | async-start | bytes 131072 | tf_op jit(solution)/shard_map/all_to_all | solution.py:217
  153.1 46.8 %all-to-all-start.2 = ((bf16[128,4,2048]{2,1,0:T(4,128)(2,1)}), bf16[128,4,2048]{2,1,0:T(4,128)(2,1)S(1)}, u32[]{:S(2)}, u32[]{:S(2)}) async-start(bf16[128,4,2048]{2,1,0:T(4,128)(2,1)} %reshape.395), calls=%async_computation.2 | async-start | bytes 4194304 | tf_op jit(solution)/shard_map/all_to_all | solution.py:210
  201.9 21.9 %copy-start.4 = (bf16[1,1,256,2048]{3,2,1,0:T(8,128)(2,1)S(1)}, bf16[1,1,256,2048]{3,2,1,0:T(8,128)(2,1)}, u32[]{:S(2)}) copy-start(bf16[1,1,256,2048]{3,2,1,0:T(8,128)(2,1)} %param.13) | copy-start | bytes 3145732
  223.8 6.0 %copy-start.8 = (f32[128]{0:T(128)S(1)}, f32[128]{0:T(128)}, u32[]{:S(2)}) copy-start(f32[128]{0:T(128)} %param.18) | copy-start | bytes 1540
  376.6 3.2 copy-start.1
Sparse Core Ops, SparseCore 0:
  22.6 52.4 all-gather.5
  77.2 51.2 all-gather.11
  130.6 93.1 all-gather.9
  225.3 32.5 all-gather.7
  259.5 32.0 all-gather.13
